TPU v7x, 256 devices: a whole 4x4x8 slice. The times are simulated.
256 devices in a mesh: row: 8 (over z), col: 32 (over y, x, core).
Axes of the slice: x: 4, y: 4, z: 8, core: 2. Of those that a mesh axis runs over, the one named last changes fastest.
Arguments:
- tiles: bfloat16 [8, 32, 16, 576, 576], P('row', 'col'), may hold values from -0.0625 to 0.0625
- diag_tiles: bfloat16 [256, 576, 576], P(('row', 'col')), as said below
- probes: float32 [256, 64, 576], P(('row', 'col'))
- rows_list: int32 [8, 32, 16], P('row', 'col'), may hold values from 0 to 31, as said below
- cols_list: int32 [8, 32, 16], P('row', 'col'), may hold values from 0 to 7, as said below
- counts: int32 [8, 32], P('row', 'col'), may hold values from 0 to 16, as said below
Outputs:
- solution: float32 [256, 64, 576], P(('row', 'col'))
- residual: float32 [256, 64, 576], P(('row', 'col'))
Inputs may be any that keep to these rules, and one draw needn't show every extreme that they name: `rows_list`: slots past a device's count hold 0; a held slot lies strictly below the diagonal. `cols_list`: slots past a device's count hold 0. `counts`: the busiest device holds 16 tiles. `diag_tiles`: each diagonal tile is symmetric positive definite: its diagonal entries are at least 4.4 and its off-diagonal part has spectral radius below about 1.
All inputs are finite; a program needn't handle non-finite values.
Results may differ from a plain program's by a relative error of at most 0.039.
Values may be sent and summed in bfloat16 or wider, within the bound.
A program may use at most 128 MiB of HBM per device.

v0:
```python
import jax
import jax.numpy as jnp
from jax import lax
from jax.sharding import PartitionSpec as P

ITERS = 2


def gram_local(left, right):
    return jnp.einsum("tpb,tqb->pq", left, right, precision=lax.Precision.HIGHEST)


def combine(coef, block):
    return jnp.einsum("pq,tpb->tqb", coef, block, precision=lax.Precision.HIGHEST)


def solve_with(matrix, rhs):
    factor = jnp.linalg.cholesky(matrix)
    middle = lax.linalg.triangular_solve(factor, rhs, left_side=True, lower=True, transpose_a=False)
    return lax.linalg.triangular_solve(factor, middle, left_side=True, lower=True, transpose_a=True)


def curvature_sum(direction, image):
    return lax.psum(gram_local(direction, image), ("row", "col"))


def apply_operator(rounded, tiles, diag_tiles, rows_list, cols_list, counts):
    row_probe = lax.all_gather(rounded, "col", axis=0, tiled=True)
    col_probe = lax.all_gather(rounded, "row", axis=0, tiled=True)
    width_p = rounded.shape[1]
    width_b = rounded.shape[2]
    own = lax.dot_general(
        rounded[0], diag_tiles[0], (((1,), (1,)), ((), ())), preferred_element_type=jnp.float32
    )

    def turn(slot, carry):
        acc_row, acc_col = carry
        local = rows_list[0, 0, slot]
        source = cols_list[0, 0, slot]
        block = tiles[0, 0, slot]
        far = col_probe[source]
        near = row_probe[local]
        fwd = lax.dot_general(
            far, block, (((1,), (1,)), ((), ())), preferred_element_type=jnp.float32
        )
        bwd = jnp.dot(near, block, preferred_element_type=jnp.float32)
        return (acc_row.at[local].add(fwd), acc_col.at[source].add(bwd))

    start = (
        jnp.zeros((row_probe.shape[0], width_p, width_b), jnp.float32),
        jnp.zeros((col_probe.shape[0], width_p, width_b), jnp.float32),
    )
    acc_row, acc_col = lax.fori_loop(0, counts[0, 0], turn, start)
    forward = lax.psum_scatter(
        acc_row.astype(jnp.bfloat16), "col", scatter_dimension=0, tiled=True
    ).astype(jnp.float32)
    mirrored = lax.psum_scatter(
        acc_col.astype(jnp.bfloat16), "row", scatter_dimension=0, tiled=True
    ).astype(jnp.float32)
    return forward + mirrored + own[None]


def body(tiles, diag_tiles, probes, rows_list, cols_list, counts):
    solution = jnp.zeros(probes.shape, jnp.float32)
    residual = probes
    direction = probes
    norm_now = lax.psum(gram_local(residual, residual), ("row", "col"))
    for step in range(ITERS):
        image = apply_operator(
            direction.astype(jnp.bfloat16), tiles, diag_tiles, rows_list, cols_list, counts
        )
        final = step + 1 == ITERS
        curv = curvature_sum(direction, image)
        alpha = solve_with(curv, norm_now)
        solution = solution + combine(alpha, direction)
        residual = residual - combine(alpha, image)
        if not final:
            norm_next = lax.psum(gram_local(residual, residual), ("row", "col"))
            beta = solve_with(norm_now, norm_next)
            direction = residual + combine(beta, direction)
            norm_now = norm_next
    return (solution, residual)


def solution(mesh):
    placed = (
        P("row", "col", None, None, None),
        P(("row", "col"), None, None),
        P(("row", "col"), None, None),
        P("row", "col", None),
        P("row", "col", None),
        P("row", "col"),
    )
    return jax.shard_map(
        body,
        mesh=mesh,
        in_specs=placed,
        out_specs=(P(("row", "col"), None, None), P(("row", "col"), None, None)),
        check_vma=False,
    )
```

profile of v0, /device:TPU:1, one launch (start us, length us, event | category | flops | bytes accessed | tf_op | source)
XLA Modules:
  0.0 993.1 jit_solution(8945101122827908853)
XLA Ops:
  7.3 1.6 convert_element_type.30
  9.0 24.3 %all_gather.12 = bf16[8,64,576]{2,1,0:T(8,128)(2,1)S(1)} all-gather(bf16[1,64,576]{2,1,0:T(8,128)(2,1)} %convert_element_type.30), channel_id=1, replica_groups=mesh['row'=8,'col'=32] {'row'}, dimensions={0}, use_global_device_ids=true | all-gather | bytes 663552 | tf_op jit(solution)/shard_map/all_gather | solution.py:29
  33.2 31.7 %all-gather.3.cloned.1.call-done = bf16[32,64,576]{2,1,0:T(8,128)(2,1)} async-done(((bf16[1,64,576]{2,1,0:T(8,128)(2,1)}), bf16[32,64,576]{2,1,0:T(8,128)(2,1)}) %all-gather.3.cloned.1.call-update) | async-done | bytes 2359312 | tf_op jit(solution)/shard_map/all_gather | solution.py:28
  64.9 2.9 broadcast.110.clone
  68.0 22.4 %while.28 = (s32[]{:T(128)}, f32[32,64,576]{2,1,0:T(8,128)}, f32[8,64,576]{2,1,0:T(8,128)S(1)}, s32[]{:T(128)}, s32[1,1,16]{2,1,0:T(1,128)S(1)}, /*index=5*/s32[...) while((s32[]{:T(128)}, f32[32,64,576]{2,1,0:T(8,128)}, ...), condition=%wide.region_3.4_spmd, body=%wide.region_0.3_spmd.sunk | while | flops 85082160 | bytes 2297161 | solution.py:53
  68.6 0.6 constant_dynamic-slice_fusion.6
  72.8 0.7 and_reduce_fusion.8
  73.5 2.7 fusion.104
  76.2 0.7 and_reduce_fusion.9
  76.9 2.0 fusion.105
  79.5 0.6 constant_dynamic-slice_fusion.6
  83.7 0.7 and_reduce_fusion.8
  84.4 2.7 fusion.104
  87.1 0.7 and_reduce_fusion.9
  87.8 2.0 fusion.105
  90.4 1.0 convert_element_type.33
  91.4 4.4 convert_element_type.31
  95.9 0.3 fusion.49
  96.3 177.0 %reduce-scatter.7.cloned.1.call-done = bf16[1,64,576]{2,1,0:T(8,128)(2,1)} async-done(((bf16[8,64,576]{2,1,0:T(8,128)(2,1)}), bf16[1,64,576]{2,1,0:T(8,128)(2,1)}) %reduce-scatter.7.cloned.1.call-update) | async-done | bytes 73744 | tf_op jit(solution)/shard_map/reduce_scatter | solution.py:57
  273.2 92.7 %reduce-scatter.5.cloned.1.call-done = bf16[1,64,576]{2,1,0:T(8,128)(2,1)} async-done(((bf16[32,64,576]{2,1,0:T(8,128)(2,1)}), bf16[1,64,576]{2,1,0:T(8,128)(2,1)}) %reduce-scatter.5.cloned.1.call-update) | async-done | bytes 73744 | tf_op jit(solution)/shard_map/reduce_scatter | solution.py:54
  365.9 1.3 fusion.37
  367.2 0.3 convolution_bitcast_fusion.10
  367.5 77.3 %all-reduce = (f32[64,64]{0,1:T(8,128)S(1)}, f32[64,64]{0,1:T(8,128)S(1)}) all-reduce(f32[64,64]{0,1:T(8,128)S(1)} %fusion.49, f32[64,64]{0,1:T(8,128)S(1)} %convolution_bitcast_fusion.10), channel_id=1, replica_groups=mesh['row'=8,'col'=32] {'row','col'}, use_global_device_ids=true, to_apply=%region_9.11 | all-reduce | flops 8192 | bytes 65536 | tf_op jit(solution)/shard_map/psum | solution.py:67
  445.1 5.8 cholesky.70
  450.9 0.6 compare_reduce_fusion.1
  451.6 0.7 fusion.55
  452.3 4.9 custom-call.15
  457.1 5.9 cholesky.59
  463.0 0.6 compare_reduce_fusion.2
  463.7 0.7 fusion.54
  464.4 4.9 custom-call.13
  469.7 0.3 fusion.33
  470.0 0.3 fusion.45
  470.3 73.9 %psum.30 = f32[64,64]{1,0:T(8,128)S(1)} all-reduce(f32[64,64]{1,0:T(8,128)S(1)} %fusion.45), channel_id=1, replica_groups=mesh['row'=8,'col'=32] {'row','col'}, use_global_device_ids=true, to_apply=%region_10.14 | all-reduce | flops 4096 | bytes 32768 | tf_op jit(solution)/shard_map/psum | solution.py:78
  544.6 1.0 fusion.72
  545.7 20.7 %all_gather.14 = bf16[8,64,576]{2,1,0:T(8,128)(2,1)S(1)} all-gather(bf16[1,64,576]{2,1,0:T(8,128)(2,1)} %get-tuple-element.197), channel_id=1, replica_groups=mesh['row'=8,'col'=32] {'row'}, dimensions={0}, use_global_device_ids=true | all-gather | bytes 663552 | tf_op jit(solution)/shard_map/all_gather | solution.py:29
  566.4 24.9 %all-gather.5.cloned.1.call-done = bf16[32,64,576]{2,1,0:T(8,128)(2,1)} async-done(((bf16[1,64,576]{2,1,0:T(8,128)(2,1)}), bf16[32,64,576]{2,1,0:T(8,128)(2,1)}) %all-gather.5.cloned.1.call-update) | async-done | bytes 2359312 | tf_op jit(solution)/shard_map/all_gather | solution.py:28
  591.3 2.9 broadcast.110
  594.4 22.4 %while.29 = (s32[]{:T(128)}, f32[32,64,576]{2,1,0:T(8,128)}, f32[8,64,576]{2,1,0:T(8,128)S(1)}, s32[]{:T(128)}, s32[1,1,16]{2,1,0:T(1,128)S(1)}, /*index=5*/s32[...) while((s32[]{:T(128)}, f32[32,64,576]{2,1,0:T(8,128)}, ...), condition=%wide.region_14.18_spmd, body=%wide.region_11.17_spmd.sunk | while | flops 85082160 | bytes 2297161 | solution.py:53
  595.0 0.6 constant_dynamic-slice_fusion.7
  599.2 0.7 and_reduce_fusion.10
  599.9 2.7 fusion.110
  602.6 0.7 and_reduce_fusion.11
  603.3 2.0 fusion.111
  605.9 0.6 constant_dynamic-slice_fusion.7
  610.1 0.7 and_reduce_fusion.10
  610.7 2.7 fusion.110
  613.5 0.7 and_reduce_fusion.11
  614.1 2.0 fusion.111
  616.8 1.0 convert_element_type.38
  617.8 4.4 convert_element_type.36
  622.2 0.3 convolution_bitcast_fusion.9
  622.6 177.1 %reduce-scatter.11.cloned.1.call-done = bf16[1,64,576]{2,1,0:T(8,128)(2,1)} async-done(((bf16[8,64,576]{2,1,0:T(8,128)(2,1)}), bf16[1,64,576]{2,1,0:T(8,128)(2,1)}) %reduce-scatter.11.cloned.1.call-update) | async-done | bytes 73744 | tf_op jit(solution)/shard_map/reduce_scatter | solution.py:57
  799.7 93.0 %reduce-scatter.9.cloned.1.call-done = bf16[1,64,576]{2,1,0:T(8,128)(2,1)} async-done(((bf16[32,64,576]{2,1,0:T(8,128)(2,1)}), bf16[1,64,576]{2,1,0:T(8,128)(2,1)}) %reduce-scatter.9.cloned.1.call-update) | async-done | bytes 73744 | tf_op jit(solution)/shard_map/reduce_scatter | solution.py:54
  892.7 1.3 fusion.39
  894.0 0.3 fusion.43
  894.3 77.4 %psum.31 = f32[64,64]{0,1:T(8,128)S(1)} all-reduce(f32[64,64]{0,1:T(8,128)S(1)} %fusion.43), channel_id=1, replica_groups=mesh['row'=8,'col'=32] {'row','col'}, use_global_device_ids=true, to_apply=%region_17.21 | all-reduce | flops 4096 | bytes 32768 | tf_op jit(solution)/shard_map/psum | solution.py:24
  971.8 5.8 cholesky.81
  977.6 0.6 compare_reduce_fusion
  978.3 0.7 fusion.56
  978.9 4.9 custom-call.17
  983.8 0.3 fusion.57
  984.3 1.0 fusion.34
  985.3 1.0 fusion.32
  (43 shorter events, 1.9 us)
Async XLA Ops:
  7.2 358.8 %copy-start = (bf16[1,576,576]{2,1,0:T(8,128)(2,1)S(1)}, bf16[1,576,576]{2,1,0:T(8,128)(2,1)}, u32[]{:S(2)}) copy-start(bf16[1,576,576]{2,1,0:T(8,128)(2,1)} %param.24) | copy-start | bytes 1990660
  7.2 60.8 %copy-start.6 = (s32[3]{0:T(128)S(1)}, s32[3]{0:T(128)}, u32[]{:S(2)}) copy-start(s32[3]{0:T(128)} %constant.124.clone.1) | copy-start | bytes 40
  7.2 60.8 %copy-start.7 = (s32[3]{0:T(128)S(1)}, s32[3]{0:T(128)}, u32[]{:S(2)}) copy-start(s32[3]{0:T(128)} %constant.127.clone.1) | copy-start | bytes 40
  7.2 60.8 %copy-start.4 = (s32[1,1,16]{2,1,0:T(1,128)S(1)}, s32[1,1,16]{2,1,0:T(1,128)}, u32[]{:S(2)}) copy-start(s32[1,1,16]{2,1,0:T(1,128)} %param.26) | copy-start | bytes 196
  7.2 60.8 %copy-start.5 = (s32[1,1,16]{2,1,0:T(1,128)S(1)}, s32[1,1,16]{2,1,0:T(1,128)}, u32[]{:S(2)}) copy-start(s32[1,1,16]{2,1,0:T(1,128)} %param.27) | copy-start | bytes 196
  7.2 57.7 %all-gather.3.cloned.1.call-start = ((), (), s32[]{:S(2)}) async-start(), calls=%async_computation.4 | async-start | bytes 2703360 | tf_op jit(solution)/shard_map/all_gather | solution.py:28
  8.9 264.3 %reduce-scatter.7.cloned.1.call-start = ((), (), s32[]{:S(2)}) async-start(), calls=%async_computation.6 | async-start | bytes 737280 | tf_op jit(solution)/shard_map/reduce_scatter | solution.py:57
  91.4 274.6 %reduce-scatter.5.cloned.1.call-start = ((), (), s32[]{:S(2)}) async-start(), calls=%async_computation.5 | async-start | bytes 2703360 | tf_op jit(solution)/shard_map/reduce_scatter | solution.py:54
  91.4 4.5 copy-start.1
  91.4 274.5 %copy-start.3 = (bf16[1,64,576]{2,1,0:T(8,128)(2,1)S(1)}, bf16[1,64,576]{2,1,0:T(8,128)(2,1)}, u32[]{:S(2)}) copy-start(bf16[1,64,576]{2,1,0:T(8,128)(2,1)} %convert_element_type.30) | copy-start | bytes 221188
  95.9 495.5 %all-gather.5.cloned.1.call-start = ((), (), s32[]{:S(2)}) async-start(), calls=%async_computation.7 | async-start | bytes 2703360 | tf_op jit(solution)/shard_map/all_gather | solution.py:28
  545.6 254.0 %reduce-scatter.11.cloned.1.call-start = ((), (), s32[]{:S(2)}) async-start(), calls=%async_computation.9 | async-start | bytes 737280 | tf_op jit(solution)/shard_map/reduce_scatter | solution.py:57
  617.8 274.9 %reduce-scatter.9.cloned.1.call-start = ((), (), s32[]{:S(2)}) async-start(), calls=%async_computation.8 | async-start | bytes 2703360 | tf_op jit(solution)/shard_map/reduce_scatter | solution.py:54
  617.8 274.9 %copy-start.2 = (bf16[1,64,576]{2,1,0:T(8,128)(2,1)S(1)}, bf16[1,64,576]{2,1,0:T(8,128)(2,1)}, u32[]{:S(2)}) copy-start(bf16[1,64,576]{2,1,0:T(8,128)(2,1)} %get-tuple-element.197) | copy-start | bytes 221188
Sparse Core Ops, SparseCore 0:
  11.2 53.7 all-gather.2
  91.5 181.6 reduce-scatter.6
  277.1 88.7 reduce-scatter.4
  545.8 45.5 all-gather.4
  617.9 181.7 reduce-scatter.10
  803.9 88.7 reduce-scatter.8
where the time goes:
time: 997 us; the launch traced here: 993 us
  waiting for transfers between devices  596 us (60%)
  blocking collectives  274 us (27%)
  other arithmetic  54 us (5%)
  matrix products  27.4 us (3%)
  loops' own time  18.2 us (2%)
  between operations  14.4 us (1%)
    reduce_scatter x2, waiting for transfers between devices, apply_operator(): lax.psum_scatter(acc_col.astype(jnp.bfloat16), 'row', scatter_dimension=0...  354 us
    reduce_scatter x2, waiting for transfers between devices, apply_operator(): lax.psum_scatter(acc_row.astype(jnp.bfloat16), 'col', scatter_dimension=0...  186 us
    psum x1, blocking collectives, curvature_sum(): return lax.psum(gram_local(direction, image), ('row', 'col'))  77.4 us
    psum x1, blocking collectives, body(): norm_now = lax.psum(gram_local(residual, residual), ('row', 'col'))  77.3 us
    psum x1, blocking collectives, body(): norm_next = lax.psum(gram_local(residual, residual), ('row', 'col'))  73.9 us
    all_gather x2, waiting for transfers between devices, apply_operator(): row_probe = lax.all_gather(rounded, 'col', axis=0, tiled=True)  56.6 us
    all_gather x2, blocking collectives, apply_operator(): col_probe = lax.all_gather(rounded, 'row', axis=0, tiled=True)  45 us
  transfers between devices with their start and end apart: 6, of which 6 were waited for; matrix products, arithmetic and copies ran while one was open for 1% of the time, Pallas kernels for 0%

commit v1 on v0

--- a/solution.py
+++ b/solution.py
@@ -75,7 +75,9 @@
         solution = solution + combine(alpha, direction)
         residual = residual - combine(alpha, image)
         if not final:
-            norm_next = lax.psum(gram_local(residual, residual), ("row", "col"))
+            block_2 = gram_local(residual, residual)
+            parts = lax.all_gather(block_2, ("row", "col"))
+            norm_next = jnp.sum(parts, axis=0)
             beta = solve_with(norm_now, norm_next)
             direction = residual + combine(beta, direction)
             norm_now = norm_next

time: 997 us -> 1030 us (1.033)
  waiting for transfers between devices: 596 us -> 702 us
  blocking collectives: 274 us -> 199 us
    all_gather x0 -> x1, waiting for transfers between devices: none -> 103 us  [body(): parts = lax.all_gather(block_2, ('row', 'col'))]
    psum x1 -> x0, blocking collectives: 73.9 us -> none  [body(): norm_next = lax.psum(gram_local(residual, residual), ('row', 'col'))]
  transfers between devices with their start and end apart: 6 -> 7, of which waited for: 6 -> 7; matrix products, arithmetic and copies ran while one was open for 1% -> 2% of each run, Pallas kernels for 0% -> 0%
where the time goes in v1:
time: 1030 us
  waiting for transfers between devices  702 us (68%)
  blocking collectives  199 us (19%)
  other arithmetic  58 us (6%)
  matrix products  28 us (3%)
  loops' own time  18.2 us (2%)
  between operations  14.4 us (1%)
    reduce_scatter x2, waiting for transfers between devices, apply_operator(): lax.psum_scatter(acc_col.astype(jnp.bfloat16), 'row', scatter_dimension=0...  354 us
    reduce_scatter x2, waiting for transfers between devices, apply_operator(): lax.psum_scatter(acc_row.astype(jnp.bfloat16), 'col', scatter_dimension=0...  186 us
    all_gather x1, waiting for transfers between devices, body(): parts = lax.all_gather(block_2, ('row', 'col'))  103 us
    psum x1, blocking collectives, curvature_sum(): return lax.psum(gram_local(direction, image), ('row', 'col'))  77.4 us
    psum x1, blocking collectives, body(): norm_now = lax.psum(gram_local(residual, residual), ('row', 'col'))  77.3 us
    all_gather x2, waiting for transfers between devices, apply_operator(): row_probe = lax.all_gather(rounded, 'col', axis=0, tiled=True)  58.2 us
    all_gather x2, blocking collectives, apply_operator(): col_probe = lax.all_gather(rounded, 'row', axis=0, tiled=True)  44.1 us
  transfers between devices with their start and end apart: 7, of which 7 were waited for; matrix products, arithmetic and copies ran while one was open for 2% of the time, Pallas kernels for 0%

profile of v1, /device:TPU:1, one launch (start us, length us, event | category | flops | bytes accessed | tf_op | source)
XLA Modules:
  0.0 1028.3 jit_solution(6147227683289681816)
XLA Ops:
  7.3 1.6 convert_element_type.30
  9.0 24.3 %all_gather.18 = bf16[8,64,576]{2,1,0:T(8,128)(2,1)S(1)} all-gather(bf16[1,64,576]{2,1,0:T(8,128)(2,1)} %convert_element_type.30), channel_id=1, replica_groups=mesh['row'=8,'col'=32] {'row'}, dimensions={0}, use_global_device_ids=true | all-gather | bytes 663552 | tf_op jit(solution)/shard_map/all_gather | solution.py:29
  33.2 31.7 %all-gather.5.cloned.1.call-done = bf16[32,64,576]{2,1,0:T(8,128)(2,1)} async-done(((bf16[1,64,576]{2,1,0:T(8,128)(2,1)}), bf16[32,64,576]{2,1,0:T(8,128)(2,1)}) %all-gather.5.cloned.1.call-update) | async-done | bytes 2359312 | tf_op jit(solution)/shard_map/all_gather | solution.py:28
  64.9 2.9 broadcast.110.clone
  68.0 22.4 %while.28 = (s32[]{:T(128)}, f32[32,64,576]{2,1,0:T(8,128)}, f32[8,64,576]{2,1,0:T(8,128)S(1)}, s32[]{:T(128)}, s32[1,1,16]{2,1,0:T(1,128)S(1)}, /*index=5*/s32[...) while((s32[]{:T(128)}, f32[32,64,576]{2,1,0:T(8,128)}, ...), condition=%wide.region_3.4_spmd, body=%wide.region_0.3_spmd.sunk | while | flops 85082160 | bytes 2297161 | solution.py:53
  68.6 0.6 constant_dynamic-slice_fusion.6
  72.8 0.7 and_reduce_fusion.8
  73.5 2.7 fusion.104
  76.2 0.7 and_reduce_fusion.9
  76.9 2.0 fusion.105
  79.5 0.6 constant_dynamic-slice_fusion.6
  83.7 0.7 and_reduce_fusion.8
  84.4 2.7 fusion.104
  87.1 0.7 and_reduce_fusion.9
  87.8 2.0 fusion.105
  90.4 1.0 convert_element_type.33
  91.4 4.4 convert_element_type.31
  95.9 0.3 fusion.49
  96.3 177.0 %reduce-scatter.7.cloned.1.call-done = bf16[1,64,576]{2,1,0:T(8,128)(2,1)} async-done(((bf16[8,64,576]{2,1,0:T(8,128)(2,1)}), bf16[1,64,576]{2,1,0:T(8,128)(2,1)}) %reduce-scatter.7.cloned.1.call-update) | async-done | bytes 73744 | tf_op jit(solution)/shard_map/reduce_scatter | solution.py:57
  273.2 92.7 %reduce-scatter.5.cloned.1.call-done = bf16[1,64,576]{2,1,0:T(8,128)(2,1)} async-done(((bf16[32,64,576]{2,1,0:T(8,128)(2,1)}), bf16[1,64,576]{2,1,0:T(8,128)(2,1)}) %reduce-scatter.5.cloned.1.call-update) | async-done | bytes 73744 | tf_op jit(solution)/shard_map/reduce_scatter | solution.py:54
  365.9 1.3 fusion.37
  367.2 0.3 convolution_bitcast_fusion.10
  367.5 77.3 %all-reduce = (f32[64,64]{0,1:T(8,128)S(1)}, f32[64,64]{0,1:T(8,128)S(1)}) all-reduce(f32[64,64]{0,1:T(8,128)S(1)} %fusion.49, f32[64,64]{0,1:T(8,128)S(1)} %convolution_bitcast_fusion.10), channel_id=1, replica_groups=mesh['row'=8,'col'=32] {'row','col'}, use_global_device_ids=true, to_apply=%region_9.11 | all-reduce | flops 8192 | bytes 65536 | tf_op jit(solution)/shard_map/psum | solution.py:67
  445.1 5.8 cholesky.59
  450.9 0.6 compare_reduce_fusion.2
  451.6 0.7 fusion.54
  452.3 4.9 custom-call.13
  457.6 0.3 fusion.33
  457.9 0.9 fusion.45
  458.9 5.8 cholesky.70
  464.8 0.6 compare_reduce_fusion.1
  465.4 0.7 fusion.55
  466.1 4.9 custom-call.15
  471.0 103.5 %all-gather.9.cloned.1.call-done = f32[16384,64]{1,0:T(8,128)} async-done(((f32[64,64]{1,0:T(8,128)}), f32[16384,64]{1,0:T(8,128)}) %all-gather.9.cloned.1.call-update) | async-done | bytes 4194320 | tf_op jit(solution)/shard_map/all_gather | solution.py:79
  574.5 4.0 reduce_sum.9
  578.9 1.0 fusion.72
  580.0 19.8 %all_gather.22 = bf16[8,64,576]{2,1,0:T(8,128)(2,1)S(1)} all-gather(bf16[1,64,576]{2,1,0:T(8,128)(2,1)} %get-tuple-element.197), channel_id=1, replica_groups=mesh['row'=8,'col'=32] {'row'}, dimensions={0}, use_global_device_ids=true | all-gather | bytes 663552 | tf_op jit(solution)/shard_map/all_gather | solution.py:29
  599.8 26.5 %all-gather.7.cloned.1.call-done = bf16[32,64,576]{2,1,0:T(8,128)(2,1)} async-done(((bf16[1,64,576]{2,1,0:T(8,128)(2,1)}), bf16[32,64,576]{2,1,0:T(8,128)(2,1)}) %all-gather.7.cloned.1.call-update) | async-done | bytes 2359312 | tf_op jit(solution)/shard_map/all_gather | solution.py:28
  626.3 2.9 broadcast.110
  629.3 22.4 %while.29 = (s32[]{:T(128)}, f32[32,64,576]{2,1,0:T(8,128)}, f32[8,64,576]{2,1,0:T(8,128)S(1)}, s32[]{:T(128)}, s32[1,1,16]{2,1,0:T(1,128)S(1)}, /*index=5*/s32[...) while((s32[]{:T(128)}, f32[32,64,576]{2,1,0:T(8,128)}, ...), condition=%wide.region_14.18_spmd, body=%wide.region_11.17_spmd.sunk | while | flops 85082160 | bytes 2297161 | solution.py:53
  630.0 0.6 constant_dynamic-slice_fusion.7
  634.1 0.7 and_reduce_fusion.10
  634.8 2.7 fusion.110
  637.5 0.7 and_reduce_fusion.11
  638.2 2.0 fusion.111
  640.9 0.6 constant_dynamic-slice_fusion.7
  645.0 0.7 and_reduce_fusion.10
  645.7 2.7 fusion.110
  648.4 0.7 and_reduce_fusion.11
  649.1 2.0 fusion.111
  651.7 1.0 convert_element_type.38
  652.8 4.4 convert_element_type.36
  657.2 0.3 convolution_bitcast_fusion.9
  657.5 177.1 %reduce-scatter.11.cloned.1.call-done = bf16[1,64,576]{2,1,0:T(8,128)(2,1)} async-done(((bf16[8,64,576]{2,1,0:T(8,128)(2,1)}), bf16[1,64,576]{2,1,0:T(8,128)(2,1)}) %reduce-scatter.11.cloned.1.call-update) | async-done | bytes 73744 | tf_op jit(solution)/shard_map/reduce_scatter | solution.py:57
  834.6 93.2 %reduce-scatter.9.cloned.1.call-done = bf16[1,64,576]{2,1,0:T(8,128)(2,1)} async-done(((bf16[32,64,576]{2,1,0:T(8,128)(2,1)}), bf16[1,64,576]{2,1,0:T(8,128)(2,1)}) %reduce-scatter.9.cloned.1.call-update) | async-done | bytes 73744 | tf_op jit(solution)/shard_map/reduce_scatter | solution.py:54
  927.8 1.3 fusion.39
  929.1 0.3 fusion.43
  929.4 77.4 %psum.23 = f32[64,64]{0,1:T(8,128)S(1)} all-reduce(f32[64,64]{0,1:T(8,128)S(1)} %fusion.43), channel_id=1, replica_groups=mesh['row'=8,'col'=32] {'row','col'}, use_global_device_ids=true, to_apply=%region_17.21 | all-reduce | flops 4096 | bytes 32768 | tf_op jit(solution)/shard_map/psum | solution.py:24
  1006.9 5.8 cholesky.81
  1012.8 0.6 compare_reduce_fusion
  1013.4 0.7 fusion.56
  1014.1 4.9 custom-call.17
  1019.4 1.0 fusion.34
  1020.4 1.0 fusion.32
  (46 shorter events, 2.2 us)
Async XLA Ops:
  7.2 358.8 %copy-start = (bf16[1,576,576]{2,1,0:T(8,128)(2,1)S(1)}, bf16[1,576,576]{2,1,0:T(8,128)(2,1)}, u32[]{:S(2)}) copy-start(bf16[1,576,576]{2,1,0:T(8,128)(2,1)} %param.24) | copy-start | bytes 1990660
  7.2 60.8 %copy-start.6 = (s32[3]{0:T(128)S(1)}, s32[3]{0:T(128)}, u32[]{:S(2)}) copy-start(s32[3]{0:T(128)} %constant.125.clone.1) | copy-start | bytes 40
  7.2 60.8 %copy-start.7 = (s32[3]{0:T(128)S(1)}, s32[3]{0:T(128)}, u32[]{:S(2)}) copy-start(s32[3]{0:T(128)} %constant.128.clone.1) | copy-start | bytes 40
  7.2 60.8 %copy-start.4 = (s32[1,1,16]{2,1,0:T(1,128)S(1)}, s32[1,1,16]{2,1,0:T(1,128)}, u32[]{:S(2)}) copy-start(s32[1,1,16]{2,1,0:T(1,128)} %param.26) | copy-start | bytes 196
  7.2 60.8 %copy-start.5 = (s32[1,1,16]{2,1,0:T(1,128)S(1)}, s32[1,1,16]{2,1,0:T(1,128)}, u32[]{:S(2)}) copy-start(s32[1,1,16]{2,1,0:T(1,128)} %param.27) | copy-start | bytes 196
  7.2 57.7 %all-gather.5.cloned.1.call-start = ((), (), s32[]{:S(2)}) async-start(), calls=%async_computation.4 | async-start | bytes 2703360 | tf_op jit(solution)/shard_map/all_gather | solution.py:28
  8.9 264.3 %reduce-scatter.7.cloned.1.call-start = ((), (), s32[]{:S(2)}) async-start(), calls=%async_computation.6 | async-start | bytes 737280 | tf_op jit(solution)/shard_map/reduce_scatter | solution.py:57
  91.4 274.6 %reduce-scatter.5.cloned.1.call-start = ((), (), s32[]{:S(2)}) async-start(), calls=%async_computation.5 | async-start | bytes 2703360 | tf_op jit(solution)/shard_map/reduce_scatter | solution.py:54
  91.4 4.5 copy-start.1
  91.4 274.5 %copy-start.3 = (bf16[1,64,576]{2,1,0:T(8,128)(2,1)S(1)}, bf16[1,64,576]{2,1,0:T(8,128)(2,1)}, u32[]{:S(2)}) copy-start(bf16[1,64,576]{2,1,0:T(8,128)(2,1)} %convert_element_type.30) | copy-start | bytes 221188
  95.9 478.6 %all-gather.9.cloned.1.call-start = ((), (), s32[]{:S(2)}) async-start(), calls=%async_computation.10 | async-start | bytes 8421376 | tf_op jit(solution)/shard_map/all_gather | solution.py:79
  458.9 167.4 %all-gather.7.cloned.1.call-start = ((), (), s32[]{:S(2)}) async-start(), calls=%async_computation.7 | async-start | bytes 2703360 | tf_op jit(solution)/shard_map/all_gather | solution.py:28
  579.9 254.7 %reduce-scatter.11.cloned.1.call-start = ((), (), s32[]{:S(2)}) async-start(), calls=%async_computation.9 | async-start | bytes 737280 | tf_op jit(solution)/shard_map/reduce_scatter | solution.py:57
  652.7 275.1 %reduce-scatter.9.cloned.1.call-start = ((), (), s32[]{:S(2)}) async-start(), calls=%async_computation.8 | async-start | bytes 2703360 | tf_op jit(solution)/shard_map/reduce_scatter | solution.py:54
  652.8 275.0 %copy-start.2 = (bf16[1,64,576]{2,1,0:T(8,128)(2,1)S(1)}, bf16[1,64,576]{2,1,0:T(8,128)(2,1)}, u32[]{:S(2)}) copy-start(bf16[1,64,576]{2,1,0:T(8,128)(2,1)} %get-tuple-element.197) | copy-start | bytes 221188
Sparse Core Ops, SparseCore 0:
  11.2 53.7 all-gather.4
  91.5 181.6 reduce-scatter.6
  277.1 88.7 reduce-scatter.4
  459.0 115.4 all-gather.8
  580.1 46.2 all-gather.6
  652.8 181.7 reduce-scatter.10
  839.0 88.7 reduce-scatter.8
